TPU v7x, 128 devices: a whole 4x4x4 slice. The times are simulated.
128 devices in a mesh: freq: 2 (over core), vs: 64 (over z, y, x).
Axes of the slice: x: 4, y: 4, z: 4, core: 2. Of those that a mesh axis runs over, the one named last changes fastest.
Arguments:
- kernel: bfloat16 [4, 2, 256, 16384], P('freq', None, None, 'vs'), may hold values from -0.03125 to 0.03125
- sources: bfloat16 [4, 2, 2048, 16384], P('freq', None, 'vs'), may hold values from -6 to 6
- observed: float32 [256, 160, 2048], P('freq', None, 'vs'), may hold values from -6 to 6
- gate_start: int32 [256], P('freq'), may hold values from 0 to 80, as said below
- gate_length: int32 [256], P('freq'), may hold values from 1 to 160
Outputs:
- gradient: bfloat16 [4, 2, 2048, 16384], P('freq', None, 'vs')
- misfit: float32 [256, 160, 2048], P('freq', None, 'vs')
Inputs may be any that keep to these rules, and one draw needn't show every extreme that they name: gate_start + gate_length <= 160 for every receiver.
All inputs are finite; a program needn't handle non-finite values.
Results may differ from a plain program's by a relative error of at most 0.0057.
Values may be sent and summed in bfloat16 or wider, within the bound.
No kernel may reach another device: no remote copies, remote signals or barrier semaphores. Data moves between devices by JAX's collectives and lax.ppermute only.
A program may use at most 128 MiB of HBM per device.

v0:
```python
import jax
import jax.numpy as jnp
from jax import lax
from jax.sharding import PartitionSpec as P

NS = 16384
RW = 256


def complex_apply(kern, model):
    form = "frs,fvs->frv"
    real_part = jnp.einsum(
        form, kern[:, 0], model[:, 0], preferred_element_type=jnp.float32
    ) - jnp.einsum(form, kern[:, 1], model[:, 1], preferred_element_type=jnp.float32)
    imag_part = jnp.einsum(
        form, kern[:, 0], model[:, 1], preferred_element_type=jnp.float32
    ) + jnp.einsum(form, kern[:, 1], model[:, 0], preferred_element_type=jnp.float32)
    return jnp.stack([real_part, imag_part], 1)


def complex_adjoint(kern, spectrum):
    form = "frv,frs->fvs"
    real_part = jnp.einsum(
        form, spectrum[:, 0], kern[:, 0], preferred_element_type=jnp.float32
    ) + jnp.einsum(form, spectrum[:, 1], kern[:, 1], preferred_element_type=jnp.float32)
    imag_part = jnp.einsum(
        form, spectrum[:, 1], kern[:, 0], preferred_element_type=jnp.float32
    ) - jnp.einsum(form, spectrum[:, 0], kern[:, 1], preferred_element_type=jnp.float32)
    factor = (NS / RW) ** 0.5
    return factor * jnp.stack([real_part, imag_part], 1)


def transform_tables(count, samples):
    sample_index = jnp.arange(samples, dtype=jnp.int32)
    bin_index = samples // 4 + jnp.arange(count, dtype=jnp.int32)
    phase = sample_index[:, None] * bin_index[None, :] % samples
    theta = 2.0 * jnp.pi / samples * phase.astype(jnp.float32)
    return (jnp.cos(theta), jnp.sin(theta))


def local(kernel, sources, observed, gate_start, gate_length):
    gathered = lax.all_gather(kernel, "vs", axis=3, tiled=True)
    forward = complex_apply(gathered, sources)
    field = forward.astype(jnp.bfloat16)
    timed = lax.all_to_all(field, "freq", split_axis=2, concat_axis=0, tiled=True)
    count = timed.shape[0]
    samples = observed.shape[1]
    cosine, sine = transform_tables(count, samples)
    scale = count ** (-0.5)
    values = timed.astype(jnp.float32)
    highest = lax.Precision.HIGHEST
    signal = scale * (
        jnp.einsum("tf,frv->rtv", cosine, values[:, 0], precision=highest)
        - jnp.einsum("tf,frv->rtv", sine, values[:, 1], precision=highest)
    )
    sample_index = jnp.arange(samples, dtype=jnp.int32)
    inside = (sample_index[None, :] >= gate_start[:, None]) & (
        sample_index[None, :] < (gate_start + gate_length)[:, None]
    )
    gate_mask = inside.astype(jnp.float32)
    misfit = gate_mask[:, :, None] * (signal - observed)
    back_real = scale * jnp.einsum("tf,rtv->frv", cosine, misfit, precision=highest)
    back_imag = -scale * jnp.einsum("tf,rtv->frv", sine, misfit, precision=highest)
    back_spectrum = jnp.stack([back_real, back_imag], 1).astype(jnp.bfloat16)
    spectral = lax.all_to_all(back_spectrum, "freq", split_axis=0, concat_axis=2, tiled=True)
    gradient = complex_adjoint(gathered, spectral).astype(jnp.bfloat16)
    return (gradient, misfit)


def solution(mesh):
    return jax.shard_map(
        local,
        mesh=mesh,
        in_specs=(
            P("freq", None, None, "vs"),
            P("freq", None, "vs", None),
            P("freq", None, "vs"),
            P("freq"),
            P("freq"),
        ),
        out_specs=(P("freq", None, "vs", None), P("freq", None, "vs")),
        check_vma=False,
    )
```

profile of v0, /device:TPU:1, one launch (start us, length us, event | category | flops | bytes accessed | tf_op | source)
XLA Modules:
  0.0 335.3 jit_solution(14792505252984407137)
XLA Ops:
  7.2 0.0 all-gather.2.cloned.1.call-start
  7.2 1.9 copy.15
  9.1 0.0 all-gather.2.cloned.1.call-update
  9.1 0.7 add.36
  9.8 0.7 fusion.41
  10.5 229.3 %all-gather.2.cloned.1.call-done = bf16[2,2,256,16384]{3,2,0,1:T(8,128)(2,1)} async-done(((bf16[2,2,256,256]{3,2,0,1:T(8,128)(2,1)}), bf16[2,2,256,16384]{3,2,0,1:T(8,128)(2,1)}) %all-gather.2.cloned.1.call-update) | async-done | bytes 33554448 | tf_op jit(solution)/shard_map/all_gather | solution.py:42
  239.8 0.0 copy-start.1
  239.8 10.0 %fusion.4 = f32[2,256,32]{1,2,0:T(8,128)S(1)} fusion(bf16[2,2,256,16384]{3,2,0,1:T(8,128)(2,1)} %all-gather.2.cloned.1.call-done, bf16[2,2,32,16384]{3,2,1,0:T(8,128)(2,1)} %param.6), kind=kOutput, calls=%fused_computation.8 | convolution fusion | flops 536870912 | bytes 18939904 | tf_op jit(solution)/shard_map/frs,fvs->frv/dot_general | solution.py:15
  249.7 0.0 copy-done.1
  249.7 8.6 %fusion.5 = f32[2,256,32]{1,2,0:T(8,128)S(1)} fusion(bf16[2,2,256,16384]{3,2,0,1:T(8,128)(2,1)} %all-gather.2.cloned.1.call-done, bf16[2,2,32,16384]{3,2,1,0:T(8,128)(2,1)S(1)} %copy-done.1), kind=kOutput, calls=%fused_computation.9 | convolution fusion | flops 536870912 | bytes 18939904 | tf_op jit(solution)/shard_map/frs,fvs->frv/dot_general | solution.py:12
  258.4 8.6 %fusion.37 = bf16[2,1,256,32]{2,3,0,1:T(8,128)(2,1)S(1)} fusion(f32[2,256,32]{1,2,0:T(8,128)S(1)} %fusion.4, bf16[2,2,32,16384]{3,2,1,0:T(8,128)(2,1)S(1)} %copy-done.1, bf16[2,2,256,16384]{3,2,0,1:T(8,128)(2,1)} %all-gather.2.cloned.1.call-done), kind=kOutput, calls=%fused_computation.35 | convolution fusion | flops 536903680 | bytes 18972672 | tf_op jit(solution)/shard_map/frs,fvs->frv/dot_general | solution.py:17
  267.0 8.6 %fusion.34 = bf16[2,1,256,32]{2,3,0,1:T(8,128)(2,1)S(1)} fusion(f32[2,256,32]{1,2,0:T(8,128)S(1)} %fusion.5, bf16[2,2,32,16384]{3,2,1,0:T(8,128)(2,1)S(1)} %copy-done.1, bf16[2,2,256,16384]{3,2,0,1:T(8,128)(2,1)} %all-gather.2.cloned.1.call-done), kind=kOutput, calls=%fused_computation.34 | convolution fusion | flops 536903680 | bytes 18972672 | tf_op jit(solution)/shard_map/frs,fvs->frv/dot_general | solution.py:14
  275.7 0.0 copy-start
  275.7 0.2 copy.18
  275.9 0.3 reshape.54
  276.2 5.6 %all_to_all.36 = bf16[2,2,8192]{2,1,0:T(2,128)(2,1)S(1)} all-to-all(bf16[2,2,8192]{2,1,0:T(2,128)(2,1)S(1)} %reshape.54), channel_id=1, replica_groups=mesh['freq'=2,'vs'=64] {'freq'}, dimensions={0} | all-to-all | bytes 131072 | tf_op jit(solution)/shard_map/all_to_all | solution.py:45
  281.8 0.2 reshape.55
  282.0 0.1 copy.19
  282.1 1.3 fusion.42
  283.5 0.0 copy-done
  283.5 3.0 fusion.9
  286.5 1.4 fusion.32
  287.9 1.4 fusion.33
  289.3 3.0 copy.24
  292.4 3.8 %all_to_all.37 = bf16[4,2,128,32]{2,3,1,0:T(8,128)(2,1)S(1)} all-to-all(bf16[4,2,128,32]{2,3,1,0:T(8,128)(2,1)S(1)} %copy.21), channel_id=1, replica_groups=mesh['freq'=2,'vs'=64] {'freq'}, dimensions={0} | all-to-all | bytes 131072 | tf_op jit(solution)/shard_map/all_to_all | solution.py:65
  296.2 0.1 copy.29
  296.4 7.3 %fusion.2 = f32[2,32,16384]{2,1,0:T(8,128)S(1)} fusion(bf16[2,2,256,16384]{3,2,0,1:T(8,128)(2,1)} %all-gather.2.cloned.1.call-done, bf16[2,2,256,32]{2,3,0,1:T(8,128)(2,1)S(1)} %all_to_all.33), kind=kOutput, calls=%fused_computation.6 | convolution fusion | flops 536870912 | bytes 21004288 | tf_op jit(solution)/shard_map/frv,frs->fvs/dot_general | solution.py:26
  303.7 7.3 %fusion.3 = f32[2,32,16384]{2,1,0:T(8,128)S(1)} fusion(bf16[2,2,256,16384]{3,2,0,1:T(8,128)(2,1)} %all-gather.2.cloned.1.call-done, bf16[2,2,256,32]{2,3,0,1:T(8,128)(2,1)S(1)} %all_to_all.33), kind=kOutput, calls=%fused_computation.7 | convolution fusion | flops 536870912 | bytes 21004288 | tf_op jit(solution)/shard_map/frv,frs->fvs/dot_general | solution.py:23
  311.0 7.3 %fusion.1 = f32[2,1,32,16384]{3,2,0,1:T(8,128)S(1)} fusion(f32[2,32,16384]{2,1,0:T(8,128)S(1)} %fusion.2, bf16[2,2,256,16384]{3,2,0,1:T(8,128)(2,1)} %all-gather.2.cloned.1.call-done, bf16[2,2,256,32]{2,3,0,1:T(8,128)(2,1)S(1)} %all_to_all.33), kind=kOutput, calls=%fused_computation.3 | convolution fusion | flops 537919488 | bytes 25198592 | tf_op jit(solution)/shard_map/frv,frs->fvs/dot_general | solution.py:28
  318.3 7.3 %fusion = f32[2,1,32,16384]{3,2,0,1:T(8,128)S(1)} fusion(f32[2,32,16384]{2,1,0:T(8,128)S(1)} %fusion.3, bf16[2,2,256,16384]{3,2,0,1:T(8,128)(2,1)} %all-gather.2.cloned.1.call-done, bf16[2,2,256,32]{2,3,0,1:T(8,128)(2,1)S(1)} %all_to_all.33), kind=kOutput, calls=%fused_computation.2 | convolution fusion | flops 537919488 | bytes 25198592 | tf_op jit(solution)/shard_map/frv,frs->fvs/dot_general | solution.py:25
  325.7 0.5 fusion.8
  326.2 2.3 copy.23
  (5 shorter events, 0.1 us)
Async XLA Ops:
  7.2 232.6 %all-gather.2.cloned.1.call-start = ((), (), s32[]{:S(2)}) async-start(), calls=%async_computation.2 | async-start | bytes 34078720 | tf_op jit(solution)/shard_map/all_gather | solution.py:42
  239.8 10.0 %copy-start.1 = (bf16[2,2,32,16384]{3,2,1,0:T(8,128)(2,1)S(1)}, bf16[2,2,32,16384]{3,2,1,0:T(8,128)(2,1)}, u32[]{:S(2)}) copy-start(bf16[2,2,32,16384]{3,2,1,0:T(8,128)(2,1)} %param.6) | copy-start | bytes 12582916
  275.7 7.8 %copy-start = (f32[128,160,32]{0,2,1:T(8,128)S(1)}, f32[128,160,32]{0,2,1:T(8,128)}, u32[]{:S(2)}) copy-start(f32[128,160,32]{0,2,1:T(8,128)} %param.7) | copy-start | bytes 7864324
Sparse Core Ops, SparseCore 0:
  11.2 228.4 all-gather.1
where the time goes:
time: 336 us; the launch traced here: 335 us
  waiting for transfers between devices  229 us (68%)
  matrix products  72.3 us (22%)
  between operations  14.2 us (4%)
  blocking collectives  9.47 us (3%)
  local copies, waits for them, and re-layouts  8.13 us (2%)
    all_gather x1, waiting for transfers between devices, local(): gathered = lax.all_gather(kernel, 'vs', axis=3, tiled=True)  229 us
    dot_general x1, matrix products, complex_apply(): jnp.einsum(form, kern[:, 0], model[:, 1], preferred_element_type=jnp.floa...  9.96 us
    dot_general x1, matrix products, complex_apply(): jnp.einsum(form, kern[:, 1], model[:, 0], preferred_element_type=jnp.floa...  8.64 us
    dot_general x1, matrix products, complex_apply(): jnp.einsum(form, kern[:, 1], model[:, 1], preferred_element_type=jnp.floa...  8.64 us
    dot_general x1, matrix products, complex_apply(): jnp.einsum(form, kern[:, 0], model[:, 0], preferred_element_type=jnp.floa...  8.62 us
    unnamed x9, local copies, waits for them, and re-layouts  7.7 us
    dot_general x1, matrix products, complex_adjoint(): jnp.einsum(form, spectrum[:, 0], kern[:, 1], preferred_element_type=jnp.f...  7.33 us
    dot_general x1, matrix products, complex_adjoint(): jnp.einsum(form, spectrum[:, 1], kern[:, 1], preferred_element_type=jnp.f...  7.33 us
  transfers between devices with their start and end apart: 1, of which 1 were waited for; matrix products, arithmetic and copies ran while one was open for 0% of the time, Pallas kernels for 0%

commit v1 on v0

--- a/solution.py
+++ b/solution.py
@@ -39,7 +39,8 @@
 
 
 def local(kernel, sources, observed, gate_start, gate_length):
-    gathered = lax.all_gather(kernel, "vs", axis=3, tiled=True)
+    parts = lax.all_gather(kernel, "vs")
+    gathered = jnp.concatenate(parts, axis=3)
     forward = complex_apply(gathered, sources)
     field = forward.astype(jnp.bfloat16)
     timed = lax.all_to_all(field, "freq", split_axis=2, concat_axis=0, tiled=True)

time: 336 us -> 352 us (1.048)
  local copies, waits for them, and re-layouts: 8.13 us -> 87.4 us
  waiting for transfers between devices: 229 us -> 166 us
    all_gather x1, waiting for transfers between devices: 229 us -> 165 us  [local(): parts = lax.all_gather(kernel, 'vs')]
    reshape x0 -> x1, local copies, waits for them, and re-layouts: none -> 49.9 us  [local(): gathered = jnp.concatenate(parts, axis=3)]
    all_gather x0 -> x1, local copies, waits for them, and re-layouts: none -> 31.3 us  [local(): parts = lax.all_gather(kernel, 'vs')]
    unnamed x9 -> x8, local copies, waits for them, and re-layouts: 7.7 us -> 5.83 us
where the time goes in v1:
time: 352 us; the launch traced here: 350 us
  waiting for transfers between devices  166 us (47%)
  local copies, waits for them, and re-layouts  87.4 us (25%)
  matrix products  72.3 us (21%)
  between operations  14.2 us (4%)
  blocking collectives  8.28 us (2%)
    all_gather x1, waiting for transfers between devices, local(): parts = lax.all_gather(kernel, 'vs')  165 us
    reshape x1, local copies, waits for them, and re-layouts, local(): gathered = jnp.concatenate(parts, axis=3)  49.9 us
    all_gather x1, local copies, waits for them, and re-layouts, local(): parts = lax.all_gather(kernel, 'vs')  31.3 us
    dot_general x1, matrix products, complex_apply(): jnp.einsum(form, kern[:, 0], model[:, 1], preferred_element_type=jnp.floa...  9.96 us
    dot_general x1, matrix products, complex_apply(): jnp.einsum(form, kern[:, 1], model[:, 1], preferred_element_type=jnp.floa...  8.64 us
    dot_general x1, matrix products, complex_apply(): jnp.einsum(form, kern[:, 1], model[:, 0], preferred_element_type=jnp.floa...  8.64 us
    dot_general x1, matrix products, complex_apply(): jnp.einsum(form, kern[:, 0], model[:, 0], preferred_element_type=jnp.floa...  8.62 us
    dot_general x1, matrix products, complex_adjoint(): jnp.einsum(form, spectrum[:, 0], kern[:, 1], preferred_element_type=jnp.f...  7.33 us
  transfers between devices with their start and end apart: 1, of which 1 were waited for; matrix products, arithmetic and copies ran while one was open for 0% of the time, Pallas kernels for 0%

profile of v1, /device:TPU:1, one launch (start us, length us, event | category | flops | bytes accessed | tf_op | source)
XLA Modules:
  0.0 350.0 jit_solution(8827043360132575053)
XLA Ops:
  7.2 0.0 all-gather.3.cloned.1.call-start
  7.2 0.7 all-gather.3.cloned.1.call-update
  7.9 0.7 add.36
  8.6 0.7 fusion.41
  9.3 165.2 %all-gather.3.cloned.1.call-done = bf16[128,2,256,256]{3,2,1,0:T(8,128)(2,1)} async-done(((bf16[2,2,256,256]{3,2,1,0:T(8,128)(2,1)}), bf16[128,2,256,256]{3,2,1,0:T(8,128)(2,1)}) %all-gather.3.cloned.1.call-update) | async-done | bytes 33554448 | tf_op jit(solution)/shard_map/all_gather | solution.py:42
  174.5 31.3 %copy.30 = bf16[64,2,2,256,256]{4,0,3,1,2:T(8,128)(2,1)} copy(bf16[64,2,2,256,256]{4,3,2,1,0:T(8,128)(2,1)} %bitcast.113) | data formatting | bytes 67108864 | tf_op jit(solution)/shard_map/all_gather | solution.py:42
  205.8 49.9 %reshape.59 = bf16[2,2,256,16384]{3,2,0,1:T(8,128)(2,1)} reshape(bf16[2,2,256,64,256]{4,3,2,0,1:T(8,128)(2,1)} %bitcast.112) | data formatting | bytes 67108864 | tf_op jit(solution)/shard_map/reshape | solution.py:43
  255.7 10.0 %fusion.4 = f32[2,256,32]{1,2,0:T(8,128)S(1)} fusion(bf16[2,2,256,16384]{3,2,0,1:T(8,128)(2,1)} %reshape.59, bf16[2,2,32,16384]{3,2,1,0:T(8,128)(2,1)} %param.6), kind=kOutput, calls=%fused_computation.9 | convolution fusion | flops 536870912 | bytes 18939904 | tf_op jit(solution)/shard_map/frs,fvs->frv/dot_general | solution.py:15
  265.6 0.0 copy-done.1
  265.6 8.6 %fusion.5 = f32[2,256,32]{1,2,0:T(8,128)S(1)} fusion(bf16[2,2,256,16384]{3,2,0,1:T(8,128)(2,1)} %reshape.59, bf16[2,2,32,16384]{3,2,1,0:T(8,128)(2,1)S(1)} %copy-done.1), kind=kOutput, calls=%fused_computation.10 | convolution fusion | flops 536870912 | bytes 18939904 | tf_op jit(solution)/shard_map/frs,fvs->frv/dot_general | solution.py:12
  274.3 8.6 %fusion.37 = bf16[2,1,256,32]{2,3,0,1:T(8,128)(2,1)S(1)} fusion(f32[2,256,32]{1,2,0:T(8,128)S(1)} %fusion.4, bf16[2,2,32,16384]{3,2,1,0:T(8,128)(2,1)S(1)} %copy-done.1, bf16[2,2,256,16384]{3,2,0,1:T(8,128)(2,1)} %reshape.59), kind=kOutput, calls=%fused_computation.36 | convolution fusion | flops 536903680 | bytes 18972672 | tf_op jit(solution)/shard_map/frs,fvs->frv/dot_general | solution.py:17
  282.9 8.6 %fusion.34 = bf16[2,1,256,32]{2,3,0,1:T(8,128)(2,1)S(1)} fusion(f32[2,256,32]{1,2,0:T(8,128)S(1)} %fusion.5, bf16[2,2,32,16384]{3,2,1,0:T(8,128)(2,1)S(1)} %copy-done.1, bf16[2,2,256,16384]{3,2,0,1:T(8,128)(2,1)} %reshape.59), kind=kOutput, calls=%fused_computation.35 | convolution fusion | flops 536903680 | bytes 18972672 | tf_op jit(solution)/shard_map/frs,fvs->frv/dot_general | solution.py:14
  291.6 0.0 copy-start
  291.6 0.2 copy.18
  291.8 0.3 reshape.63
  292.1 4.4 %all_to_all.36 = bf16[2,2,8192]{2,1,0:T(2,128)(2,1)S(1)} all-to-all(bf16[2,2,8192]{2,1,0:T(2,128)(2,1)S(1)} %reshape.63), channel_id=1, replica_groups=mesh['freq'=2,'vs'=64] {'freq'}, dimensions={0} | all-to-all | bytes 131072 | tf_op jit(solution)/shard_map/all_to_all | solution.py:46
  296.5 0.2 reshape.64
  296.7 0.1 copy.19
  296.8 1.3 fusion.42
  298.2 0.0 copy-done
  298.2 3.0 fusion.9
  301.2 1.4 fusion.32
  302.6 1.4 fusion.33
  304.0 3.0 copy.24
  307.1 3.8 %all_to_all.37 = bf16[4,2,128,32]{2,3,1,0:T(8,128)(2,1)S(1)} all-to-all(bf16[4,2,128,32]{2,3,1,0:T(8,128)(2,1)S(1)} %copy.21), channel_id=1, replica_groups=mesh['freq'=2,'vs'=64] {'freq'}, dimensions={0} | all-to-all | bytes 131072 | tf_op jit(solution)/shard_map/all_to_all | solution.py:66
  310.9 0.1 copy.31
  311.1 7.3 %fusion.2 = f32[2,32,16384]{2,1,0:T(8,128)S(1)} fusion(bf16[2,2,256,16384]{3,2,0,1:T(8,128)(2,1)} %reshape.59, bf16[2,2,256,32]{2,3,0,1:T(8,128)(2,1)S(1)} %all_to_all.33), kind=kOutput, calls=%fused_computation.7 | convolution fusion | flops 536870912 | bytes 21004288 | tf_op jit(solution)/shard_map/frv,frs->fvs/dot_general | solution.py:26
  318.4 7.3 %fusion.3 = f32[2,32,16384]{2,1,0:T(8,128)S(1)} fusion(bf16[2,2,256,16384]{3,2,0,1:T(8,128)(2,1)} %reshape.59, bf16[2,2,256,32]{2,3,0,1:T(8,128)(2,1)S(1)} %all_to_all.33), kind=kOutput, calls=%fused_computation.8 | convolution fusion | flops 536870912 | bytes 21004288 | tf_op jit(solution)/shard_map/frv,frs->fvs/dot_general | solution.py:23
  325.7 7.3 %fusion.1 = f32[2,1,32,16384]{3,2,0,1:T(8,128)S(1)} fusion(f32[2,32,16384]{2,1,0:T(8,128)S(1)} %fusion.2, bf16[2,2,256,16384]{3,2,0,1:T(8,128)(2,1)} %reshape.59, bf16[2,2,256,32]{2,3,0,1:T(8,128)(2,1)S(1)} %all_to_all.33), kind=kOutput, calls=%fused_computation.4 | convolution fusion | flops 537919488 | bytes 25198592 | tf_op jit(solution)/shard_map/frv,frs->fvs/dot_general | solution.py:28
  333.0 7.3 %fusion = f32[2,1,32,16384]{3,2,0,1:T(8,128)S(1)} fusion(f32[2,32,16384]{2,1,0:T(8,128)S(1)} %fusion.3, bf16[2,2,256,16384]{3,2,0,1:T(8,128)(2,1)} %reshape.59, bf16[2,2,256,32]{2,3,0,1:T(8,128)(2,1)S(1)} %all_to_all.33), kind=kOutput, calls=%fused_computation.3 | convolution fusion | flops 537919488 | bytes 25198592 | tf_op jit(solution)/shard_map/frv,frs->fvs/dot_general | solution.py:25
  340.4 0.5 fusion.8
  340.9 2.3 copy.23
  (6 shorter events, 0.1 us)
Async XLA Ops:
  7.2 167.3 %all-gather.3.cloned.1.call-start = ((), (), s32[]{:S(2)}) async-start(), calls=%async_computation.2 | async-start | bytes 34078720 | tf_op jit(solution)/shard_map/all_gather | solution.py:42
  255.7 10.0 %copy-start.1 = (bf16[2,2,32,16384]{3,2,1,0:T(8,128)(2,1)S(1)}, bf16[2,2,32,16384]{3,2,1,0:T(8,128)(2,1)}, u32[]{:S(2)}) copy-start(bf16[2,2,32,16384]{3,2,1,0:T(8,128)(2,1)} %param.6) | copy-start | bytes 12582916
  291.6 6.6 %copy-start = (f32[128,160,32]{0,2,1:T(8,128)S(1)}, f32[128,160,32]{0,2,1:T(8,128)}, u32[]{:S(2)}) copy-start(f32[128,160,32]{0,2,1:T(8,128)} %param.7) | copy-start | bytes 7864324
Sparse Core Ops, SparseCore 0:
  10.8 163.6 all-gather.2
